TPU v7x, 32 devices: a whole 2x2x4 slice. The times are simulated.
32 devices in a mesh: groups: 2 (over y), rec: 4 (over z), attr: 4 (over x, core).
Axes of the slice: x: 2, y: 2, z: 4, core: 2. Of those that a mesh axis runs over, the one named last changes fastest.
Arguments:
- cells: bfloat16 [64, 49152], P(('groups', 'rec'), 'attr'), parts along dimension 0, may hold values from -1000 to 1000
- cotangent: bfloat16 [64, 49152], P(('groups', 'rec'), 'attr'), parts along dimension 0, may hold values from -6 to 6
- qkv_attr: bfloat16 [192, 576], replicated, may hold values from -8 to 8
- out_attr: bfloat16 [192, 192], replicated, may hold values from -0.4375 to 0.4375
- qkv_samp: bfloat16 [192, 576], replicated, may hold values from -8 to 8
- out_samp: bfloat16 [192, 192], replicated, may hold values from -0.4375 to 0.4375
- up_weight: bfloat16 [192, 768], replicated, may hold values from -0.4375 to 0.4375
- down_weight: bfloat16 [768, 192], replicated, may hold values from -0.21875 to 0.21875
- train_split: int32 [64], P('groups'), parts along dimension 0, may hold values from 0 to 1, as said below
Outputs:
- grad_cells: bfloat16 [64, 49152], P(('groups', 'rec'), 'attr'), parts along dimension 0
- grad_qkv_attr: float32 [384, 576], P('groups'), parts along dimension 0
- grad_out_attr: float32 [384, 192], P('groups'), parts along dimension 0
- grad_qkv_samp: float32 [384, 576], P('groups'), parts along dimension 0
- grad_out_samp: float32 [384, 192], P('groups'), parts along dimension 0
- grad_up: float32 [384, 768], P('groups'), parts along dimension 0
- grad_down: float32 [1536, 192], P('groups'), parts along dimension 0
There are 2 independent parts, one for each index of `groups`. A program takes and returns all parts, laid end to end along the dimension named above; an argument that names none is the same for every part. Nothing has to cross between parts.
Inputs may be any that keep to these rules, and one draw needn't show every extreme that they name: `train_split`: every table window has at least one training record.
All inputs are finite; a program needn't handle non-finite values.
Results may differ from a plain program's by a relative error of at most 0.018.
The roundings to bfloat16 on the way count: a program that leaves them out, or rounds other values in their place, can miss the bound.
Values may be sent and summed in bfloat16 or wider, within the bound.
A program may use at most 64 MiB of HBM per device.

v0:
```python
import functools
import math

import jax
import jax.numpy as jnp
import numpy as np
from jax import lax
from jax.experimental import pallas as pl
from jax.experimental.pallas import tpu as pltpu
from jax.sharding import PartitionSpec as P

E = 192
HEADS = 6
HD = E // HEADS
SCALE = 1.0 / math.sqrt(HD)
BLOCKS = 16
F32 = jnp.float32
BF16 = jnp.bfloat16
MESH = pl.DeviceIdType.MESH
NN = (((1,), (0,)), ((), ()))
NT = (((1,), (1,)), ((), ()))
TN = (((0,), (0,)), ((), ()))
VMEM = pl.BlockSpec(memory_space=pltpu.VMEM)
ANY = pl.BlockSpec(memory_space=pl.ANY)
HBM = pl.BlockSpec(memory_space=pltpu.HBM)


def dot(a, b, form=NN):
    return lax.dot_general(a, b, form, preferred_element_type=F32)


def place(sizes, order):
    index = np.arange(math.prod(sizes)).reshape(sizes).transpose(order).reshape(-1)
    there = np.empty_like(index)
    there[index] = np.arange(index.size)
    return there.astype(np.int32)


def moved(where_ref, x):
    n = x.shape[0]
    hot = lax.broadcasted_iota(jnp.int32, (n, n), 0) == where_ref[...]
    return dot(jnp.where(hot, 1.0, 0.0).astype(BF16), x)


def put(ref, b, value):
    pieces, part = ref.shape[1], ref.shape[2]
    side = jnp.concatenate([value[: E // 2], value[E // 2:]], axis=1)
    for r in range(pieces):
        ref[b, r] = side[r * part:(r + 1) * part].astype(BF16)


def pack(ref, value, few):
    run = value.shape[0] // few
    pieces, part = ref.shape[0], ref.shape[1]
    side = jnp.concatenate([value[k * run:(k + 1) * run] for k in range(few)], axis=1)
    for r in range(pieces):
        ref[r] = side[r * part:(r + 1) * part].astype(BF16)


def unpack(ref, flat, few):
    pieces, part = ref.shape[0], ref.shape[1]
    run = pieces * part
    for r in range(pieces):
        side = ref[r].astype(F32)
        for k in range(few):
            flat[k * run + r * part:k * run + (r + 1) * part] = side[:, k * E:(k + 1) * E]
    return flat[...].astype(BF16)


def norm(x):
    center = x - jnp.mean(x, axis=-1, keepdims=True)
    scale = lax.rsqrt(jnp.mean(center * center, axis=-1, keepdims=True) + 1e-05)
    return center * scale, scale


def norm_back(hat, scale, grad):
    return scale * (
        grad
        - jnp.mean(grad, axis=-1, keepdims=True)
        - hat * jnp.mean(grad * hat, axis=-1, keepdims=True)
    )


def attend(x_ref, qkv, out, qkv_s, p_s, acc, n, size, bias):
    normed = norm(x_ref[...].astype(F32))[0].astype(BF16)
    for t in range(3):
        qkv_s[t] = dot(normed, qkv[:, t * E:(t + 1) * E]).T.astype(BF16)

    def head(h, _):
        rows = pl.ds(pl.multiple_of(h * HD, HD), HD)
        for b in range(n):
            cols = pl.ds(b * size, size)
            s = dot(qkv_s[1, rows, cols], qkv_s[0, rows, cols], TN) * SCALE
            if bias is not None:
                s = jnp.where(bias[...] > 0, s, -1e30)
            e = jnp.exp(s - jnp.max(s, axis=0, keepdims=True))
            p = e * (1.0 / jnp.sum(e, axis=0, keepdims=True))
            p_s[b, h] = p
            acc[0, rows, cols] = dot(qkv_s[2, rows, cols], p.astype(BF16))
        return 0

    lax.fori_loop(0, HEADS, head, 0)
    mixed = acc[0].T.astype(BF16)
    return normed, mixed, (x_ref[...].astype(F32) + dot(mixed, out)).astype(BF16)


def attend_back(x, g, mixed, qkv, out, qkv_s, p_s, acc, dm_s, grads, first, n, size, between):
    dm_s[...] = dot(out, g, NT).astype(BF16)
    put(grads, first + 3, dot(mixed, g, TN))

    def head(h, _):
        rows = pl.ds(pl.multiple_of(h * HD, HD), HD)
        for b in range(n):
            cols = pl.ds(b * size, size)
            dm = dm_s[rows, cols]
            p = p_s[b, h]
            dp = dot(qkv_s[2, rows, cols], dm, TN).astype(BF16).astype(F32)
            ds = (p * (dp - jnp.sum(dp * p, axis=0, keepdims=True)) * SCALE).astype(BF16)
            acc[0, rows, cols] = dot(qkv_s[1, rows, cols], ds)
            acc[1, rows, cols] = dot(qkv_s[0, rows, cols], ds, NT)
            acc[2, rows, cols] = dot(dm, p.astype(BF16), NT)
        return 0

    for k, step in enumerate(between):
        lax.fori_loop(k * HEADS // len(between), (k + 1) * HEADS // len(between), head, 0)
        step()
    hat, scale = norm(x.astype(F32))
    normed = hat.astype(BF16)
    dn = None
    for t in range(3):
        d = acc[t].T.astype(BF16)
        put(grads, first + t, dot(normed, d, TN))
        part = dot(d, qkv[:, t * E:(t + 1) * E], NT)
        dn = part if dn is None else dn + part
    return (g.astype(F32) + norm_back(hat, scale, dn.astype(BF16).astype(F32))).astype(BF16)


def rows_of(cells, flat):
    rows = cells.shape[0]
    for a in range(cells.shape[1] // E):
        flat[a * rows:(a + 1) * rows] = cells[:, a * E:(a + 1) * E].astype(F32)
    return flat[...].astype(BF16)


def shifts_of(axes):
    sizes = [lax.axis_size(a) for a in axes]
    return [s for s in np.ndindex(*sizes) if any(s)], sizes


def peers_of(axes):
    shifts, sizes = shifts_of(axes)
    me = [lax.axis_index(a) for a in axes]
    return [[lax.rem(m + d, n) for m, d, n in zip(me, s, sizes)] for s in shifts]


def start_swap(axes, src, dst, sems):
    _, sizes = shifts_of(axes)

    def flat(where):
        number = where[0]
        for w, n in zip(where[1:], sizes[1:]):
            number = number * n + w
        return number

    me = flat([lax.axis_index(a) for a in axes])
    copies = []
    for k, to in enumerate(peers_of(axes)):
        copy = pltpu.make_async_remote_copy(
            src_ref=src.at[flat(to)],
            dst_ref=dst.at[me],
            send_sem=sems.at[0, k],
            recv_sem=sems.at[1, k],
            device_id=dict(zip(axes, to)),
            device_id_type=MESH,
        )
        copy.start()
        copies.append(copy)
    dst[me] = src[me]
    return copies


def settle(copies):
    for copy in copies:
        copy.wait()


def total_steps(buf, out, first, count, r1, r2, r3, s1, s2, sems):
    rec, attr = lax.axis_index("rec"), lax.axis_index("attr")
    n_rec, n_x = lax.axis_size("rec"), lax.axis_size("attr") // 2
    half, x = lax.rem(attr, 2), lax.div(attr, 2)
    h1 = count // 2
    h2 = h1 // n_x
    base = first + half * h1 + x * h2
    sem = iter(range(sems.shape[1]))

    def push(src, dst, device):
        k = next(sem)
        copy = pltpu.make_async_remote_copy(
            src_ref=src, dst_ref=dst, send_sem=sems.at[0, k], recv_sem=sems.at[1, k],
            device_id=device, device_id_type=MESH,
        )
        copy.start()
        return copy

    partner = {"attr": x * 2 + 1 - half}
    columns = [lax.rem(x + d, n_x) for d in range(1, n_x)]
    lines = [lax.rem(rec + d, n_rec) for d in range(1, n_rec)]
    copies = [push(buf.at[pl.ds(first + (1 - half) * h1, h1)], r1, partner)]
    yield
    settle(copies)
    for b in range(h1):
        s1[b] = (buf[first + half * h1 + b].astype(F32) + r1[b].astype(F32)).astype(BF16)
    copies = [
        push(s1.at[pl.ds(c * h2, h2)], r2.at[d], {"attr": c * 2 + half}) for d, c in enumerate(columns)
    ]
    yield
    settle(copies)
    for b in range(h2):
        value = s1[x * h2 + b].astype(F32)
        for d in range(n_x - 1):
            value += r2[d, b].astype(F32)
        s2[b] = value.astype(BF16)
    copies = [push(s2.at[:, r], r3.at[d], {"rec": r}) for d, r in enumerate(lines)]
    yield
    settle(copies)
    for b in range(h2):
        value = s2[b, rec].astype(F32)
        for d in range(n_rec - 1):
            value += r3[d, b].astype(F32)
        out[base + b, rec] = value.astype(BF16)
    own = out.at[pl.ds(base, h2), rec]
    copies = [push(own, own, {"rec": r}) for r in lines]
    yield
    settle(copies)
    own = out.at[pl.ds(base, h2)]
    copies = [push(own, own, {"attr": c * 2 + half}) for c in columns]
    yield
    settle(copies)
    own = out.at[pl.ds(first + half * h1, h1)]
    copies = [push(own, own, partner)]
    yield
    settle(copies)
    yield


COUNTS = (8, 4, 4)


def layer_kernel(
    size_a, size_s, length, few,
    cells_h, cot_h, qkva_h, outa_h, qkvs_h, outs_h, up_h, down_h, split_h, place_h,
    o_got, totals,
    cells, cot, qkva, outa, qkvs, outs, up, down, split, places, in_sems,
    flat, c_send, c_got, g_send, g_got, f_send, f_got, b_send, b_got, o_send,
    x_a, mixed_a, qkv_a, p_a, x_s, g_s, qkv_s, p_s, acc, dm_s, dn_s, bias, grads,
    c_sems, g_sems, f_sems, b_sems, o_sems, *sums,
):
    tokens = flat.shape[0]
    n_a, n_s = tokens // size_a, tokens // size_s
    loads = {}
    pairs = (
        (cells_h, cells), (place_h, places), (cot_h, cot), (qkva_h, qkva), (outa_h, outa),
        (split_h, split), (qkvs_h, qkvs), (outs_h, outs), (up_h, up), (down_h, down),
    )
    for k, (src, dst) in enumerate(pairs):
        loads[k] = pltpu.make_async_copy(src, dst, in_sems.at[k])
        loads[k].start()
    barrier = pltpu.get_barrier_semaphore()
    peers = peers_of(("rec", "attr"))
    for r, a in peers:
        pl.semaphore_signal(barrier, inc=1, device_id={"rec": r, "attr": a}, device_id_type=MESH)

    def at(k):
        return places.at[k:k + 1]

    loads[0].wait()
    loads[1].wait()
    pack(c_send, moved(at(0), rows_of(cells, flat)), few)
    pl.semaphore_wait(barrier, len(peers))
    c_copies = start_swap(("attr",), c_send, c_got, c_sems)
    loads[2].wait()
    pack(g_send, moved(at(1), rows_of(cot, flat)), few)
    g_copies = start_swap(("rec",), g_send, g_got, g_sems)
    for k in range(3, len(pairs)):
        loads[k].wait()
    settle(c_copies)
    x_a[...] = unpack(c_got, flat, few)
    _, mixed, first = attend(x_a, qkva, outa[...], qkv_a, p_a, acc, n_a, size_a, None)
    mixed_a[...] = mixed
    pack(f_send, moved(at(2), first), few)
    f_copies = start_swap(("rec", "attr"), f_send, f_got, f_sems)

    row = lax.broadcasted_iota(jnp.int32, (size_s, size_s), 0)
    column = lax.broadcasted_iota(jnp.int32, (size_s, size_s), 1)
    same = None
    for s in range(size_s // length):
        low, high = s * length, (s + 1) * length
        inside = (row >= low) & (row < high) & (column >= low) & (column < high)
        same = inside if same is None else same | inside
    tiled = jnp.concatenate([split[...].astype(F32)] * (size_s // length), axis=1)
    bias[...] = jnp.where(same, tiled, 0.0).T
    settle(g_copies)
    g_s[...] = moved(at(4), unpack(g_got, flat, few)).astype(BF16)
    settle(f_copies)
    x_s[...] = moved(at(3), unpack(f_got, flat, few)).astype(BF16)
    _, mixed, second = attend(x_s, qkvs, outs[...], qkv_s, p_s, acc, n_s, size_s, bias)
    hat, scale = norm(second.astype(F32))
    normed = hat.astype(BF16)
    g = g_s[...]
    for c in range(up.shape[1] // E):
        w_up = up[:, c * E:(c + 1) * E]
        pre = dot(normed, w_up)
        cdf = 0.5 * (1.0 + lax.erf(pre * (1.0 / math.sqrt(2.0))))
        hidden = (pre * cdf).astype(BF16)
        slope = cdf + pre * (jnp.exp(pre * pre * -0.5) * (1.0 / math.sqrt(2.0 * math.pi)))
        dh = dot(g, down[:, c * E:(c + 1) * E]).astype(BF16).astype(F32)
        dpre = (dh * slope).astype(BF16)
        put(grads, c, dot(normed, dpre, TN))
        put(grads, 4 + c, dot(g, hidden, TN))
        part = dot(dpre, w_up, NT)
        if c == 0:
            dn_s[...] = part
        else:
            dn_s[...] += part
    starts = (0, COUNTS[0], COUNTS[0] + COUNTS[1])
    ffn, samp, attr = (
        total_steps(grads, totals, starts[k], COUNTS[k], *sums[6 * k:6 * k + 6]) for k in range(3)
    )
    next(ffn)
    dn = dn_s[...].astype(BF16).astype(F32)
    g = (g.astype(F32) + norm_back(hat, scale, dn)).astype(BF16)

    def go(*groups):
        def step():
            for group in groups:
                next(group)
        return step

    back = attend_back(
        x_s[...], g, mixed, qkvs, outs[...], qkv_s, p_s, acc, dm_s, grads, starts[1], n_s, size_s,
        (go(ffn), go(), go(ffn)),
    )
    pack(b_send, moved(at(5), back), few)
    b_copies = start_swap(("rec", "attr"), b_send, b_got, b_sems)
    next(samp)
    settle(b_copies)
    go(samp, ffn)()
    g = moved(at(6), unpack(b_got, flat, few)).astype(BF16)
    back = attend_back(
        x_a[...], g, mixed_a[...], qkva, outa[...], qkv_a, p_a, acc, dm_s, grads, starts[2], n_a, size_a,
        (go(ffn), go(samp), go(ffn)),
    )
    next(attr)
    pack(o_send, back.astype(F32), few)
    o_copies = start_swap(("attr",), o_send, o_got, o_sems)
    for steps in (samp, attr, ffn, samp, attr, samp, attr, samp, attr, attr, attr):
        next(steps)
    settle(o_copies)


def finish_kernel(
    factor, few, tokens_h, places_h, total_h, cells, qa, oa, qs, os, gu, gd,
    tokens, places, total, sems, flat, out_flat, tmp,
):
    loads = [
        pltpu.make_async_copy(src, dst, sems.at[k])
        for k, (src, dst) in enumerate(((tokens_h, tokens), (places_h, places), (total_h, total)))
    ]
    for load in loads:
        load.start()
    rows = cells.shape[0]
    loads[0].wait()
    loads[1].wait()
    out_flat[...] = moved(places.at[7:8], unpack(tokens, flat, few))
    for a in range(0, cells.shape[1] // E, 2):
        pair = [out_flat[(a + k) * rows:(a + k + 1) * rows] for k in range(2)]
        cells[:, a * E:(a + 2) * E] = jnp.concatenate(pair, axis=1).astype(BF16)
    loads[2].wait()

    def block(b):
        part = total.shape[2]
        for r in range(total.shape[1]):
            tmp[b, r * part:(r + 1) * part] = total[b, r].astype(F32) * factor
        side = tmp[b]
        return jnp.concatenate([side[:, :E], side[:, E:]], axis=0)

    gu[...] = jnp.concatenate([block(c) for c in range(4)], axis=1)
    gd[...] = jnp.concatenate([block(4 + c) for c in range(4)], axis=1)
    for ref, start in ((qs, 8), (qa, 12)):
        ref[...] = jnp.concatenate([block(start + t) for t in range(3)], axis=1)
    os[...] = block(11)
    oa[...] = block(15)


def local(
    cells, cotangent, qkv_attr, out_attr, qkv_samp, out_samp, up_weight, down_weight, train_split
):
    n_rec, n_attr = lax.axis_size("rec"), lax.axis_size("attr")
    rows, cols = cells.shape[0], cells.shape[1] // E
    tokens = rows * cols
    width = cols * n_attr
    length = rows * n_rec
    few = rows // n_attr
    thin = cols // n_rec
    size = length * max(1, min(256 // length, thin))
    places = jnp.asarray(np.stack([
        place((cols, n_attr, few), (2, 1, 0)),
        place((n_rec, thin, n_attr, few), (3, 0, 1, 2)),
        place((few, n_attr, n_rec, thin), (0, 2, 1, 3)),
        place((few, n_rec, n_attr, thin), (3, 1, 2, 0)),
        place((few, n_rec, thin, n_attr), (2, 1, 3, 0)),
        place((thin, n_rec, n_attr, few), (3, 1, 2, 0)),
        place((few, n_rec, n_attr, thin), (0, 2, 1, 3)),
        place((few, n_attr, cols), (2, 1, 0)),
    ]))
    split = train_split[None, :]
    all_devices = n_rec * n_attr
    part = E // 2 // n_rec
    n_x = n_attr // 2

    def shape(*dims, dtype=BF16):
        return jax.ShapeDtypeStruct(dims, dtype)

    def vmem(*dims, dtype=BF16):
        return pltpu.VMEM(dims, dtype)

    args = (
        cells, cotangent, qkv_attr, out_attr, qkv_samp, out_samp, up_weight, down_weight.T, split, places
    )
    c_buf = vmem(n_attr, cols, few * E)
    g_buf = vmem(n_rec, thin * n_attr, few * E)
    f_buf = vmem(all_devices, thin, few * E)
    table = vmem(tokens, E)
    sums = []
    for count in COUNTS:
        h1 = count // 2
        h2 = h1 // n_x
        sums += [
            vmem(h1, n_rec, part, 2 * E), vmem(max(1, n_x - 1), h2, n_rec, part, 2 * E),
            vmem(max(1, n_rec - 1), h2, part, 2 * E), vmem(h1, n_rec, part, 2 * E),
            vmem(h2, n_rec, part, 2 * E),
            pltpu.SemaphoreType.DMA((2, 2 * (n_rec + n_x - 1))),
        ]
    o_got, totals = pl.pallas_call(
        functools.partial(layer_kernel, width, size, length, few),
        out_shape=[shape(n_attr, cols, few * E), shape(BLOCKS, n_rec, part, 2 * E)],
        in_specs=[HBM] * len(args),
        out_specs=[VMEM] * 2,
        scratch_shapes=[pltpu.VMEM(a.shape, a.dtype) for a in args]
        + [
            pltpu.SemaphoreType.DMA((len(args),)),
            vmem(tokens, E, dtype=F32), c_buf, c_buf, g_buf, g_buf, f_buf, f_buf, f_buf, f_buf, c_buf,
            table, table, vmem(3, E, tokens), vmem(tokens // width, HEADS, width, width, dtype=F32),
            table, table, vmem(3, E, tokens), vmem(tokens // size, HEADS, size, size, dtype=F32),
            vmem(3, E, tokens, dtype=F32), vmem(E, tokens), vmem(tokens, E, dtype=F32),
            vmem(size, size, dtype=F32), vmem(BLOCKS, n_rec, part, 2 * E),
        ]
        + [
            pltpu.SemaphoreType.DMA((2, n))
            for n in (n_attr, n_rec, all_devices, all_devices, n_attr)
        ]
        + sums,
        compiler_params=pltpu.CompilerParams(
            collective_id=0, has_side_effects=True, vmem_limit_bytes=67043328
        ),
    )(*args)
    outs = [
        shape(rows, cols * E), shape(E, 3 * E, dtype=F32), shape(E, E, dtype=F32),
        shape(E, 3 * E, dtype=F32), shape(E, E, dtype=F32),
        shape(E, 4 * E, dtype=F32), shape(E, 4 * E, dtype=F32),
    ]
    last = (o_got, places, totals)
    out = pl.pallas_call(
        functools.partial(finish_kernel, 1.0 / math.sqrt(length * width), few),
        out_shape=outs,
        in_specs=[ANY] * 3,
        out_specs=[VMEM] * len(outs),
        scratch_shapes=[pltpu.VMEM(a.shape, a.dtype) for a in last]
        + [
            pltpu.SemaphoreType.DMA((3,)), vmem(tokens, E, dtype=F32), vmem(tokens, E, dtype=F32),
            vmem(BLOCKS, E // 2, 2 * E, dtype=F32),
        ],
        compiler_params=pltpu.CompilerParams(vmem_limit_bytes=67043328),
    )(*last)
    return (*out[:6], out[6].T)


def solution(mesh):
    both = P(("groups", "rec"), "attr")
    in_specs = (both, both, P(), P(), P(), P(), P(), P(), P("groups"))
    out_specs = (both,) + (P("groups", None),) * 6
    return jax.shard_map(local, mesh=mesh, in_specs=in_specs, out_specs=out_specs, check_vma=False)
```

profile of v0, /device:TPU:0, one launch (start us, length us, event | category | flops | bytes accessed | tf_op | source)
XLA Modules:
  0.0 81.4 jit_solution(15673744628629907534)
XLA Ops:
  0.6 77.3 %shard_map.153 = (bf16[4,64,384]{2,1,0:T(8,128)(2,1)}, bf16[16,4,24,384]{3,2,1,0:T(8,128)(2,1)}) custom-call(bf16[8,12288]{1,0:T(8,128)(2,1)} %cells_h.1, bf16[8,12288]{1,0:T(8,128)(2,1)} %cot_h.1, bf16[192,576]{1,0:T(8,128)(2,1)} %qkva_h.1, bf16[192,192]{1,0:T(8,128)(2,1)} %outa_h.1, bf16[192,576]{1,0:T(8,128)(2,1)} %qkvs_h.1, bf16[192,192]{1,0:T(8,128)(2,1)} %outs_h.1, ...), custom_call_target="tpu_custom_call" | custom-call | tf_op jit(solution)/shard_map/pallas_call | solution.py:444
  78.0 3.2 %shard_map.154 = (bf16[8,12288]{1,0:T(8,128)(2,1)}, f32[192,576]{1,0:T(8,128)}, f32[192,192]{1,0:T(8,128)}, f32[192,576]{1,0:T(8,128)}, f32[192,192]{1,0:T(8,128...) custom-call(bf16[4,64,384]{2,1,0:T(8,128)(2,1)} %get-tuple-element.16.tokens_h, s32[8,512]{1,0:T(8,128)} %constant.2.clone.place_h.places_h, ...), custom_call_target="tpu_custom_call" | custom-call | tf_op jit(solution)/shard_map/pallas_call | solution.py:473
where the time goes:
time: 81.5 us; the launch traced here: 81.4 us
  Pallas kernels  80.6 us (99%)
    pallas_call x1, Pallas kernels, local(): pl.pallas_call(functools.partial(layer_kernel, width, size, length, few),...  77.3 us
    pallas_call x1, Pallas kernels, local(): pl.pallas_call(functools.partial(finish_kernel, 1.0 / math.sqrt(length *...  3.25 us

commit v1 on v0

--- a/solution.py
+++ b/solution.py
@@ -86,8 +86,8 @@
     for t in range(3):
         qkv_s[t] = dot(normed, qkv[:, t * E:(t + 1) * E]).T.astype(BF16)
 
-    def head(h, _):
-        rows = pl.ds(pl.multiple_of(h * HD, HD), HD)
+    def head(h):
+        rows = pl.ds(h * HD, HD)
         for b in range(n):
             cols = pl.ds(b * size, size)
             s = dot(qkv_s[1, rows, cols], qkv_s[0, rows, cols], TN) * SCALE
@@ -97,19 +97,18 @@
             p = e * (1.0 / jnp.sum(e, axis=0, keepdims=True))
             p_s[b, h] = p
             acc[0, rows, cols] = dot(qkv_s[2, rows, cols], p.astype(BF16))
-        return 0
-
-    lax.fori_loop(0, HEADS, head, 0)
+
+    for h in range(HEADS):
+        head(h)
     mixed = acc[0].T.astype(BF16)
     return normed, mixed, (x_ref[...].astype(F32) + dot(mixed, out)).astype(BF16)
 
 
-def attend_back(x, g, mixed, qkv, out, qkv_s, p_s, acc, dm_s, grads, first, n, size, between):
+def heads_back(g, out, qkv_s, p_s, acc, dm_s, n, size, between):
     dm_s[...] = dot(out, g, NT).astype(BF16)
-    put(grads, first + 3, dot(mixed, g, TN))
-
-    def head(h, _):
-        rows = pl.ds(pl.multiple_of(h * HD, HD), HD)
+
+    def head(h):
+        rows = pl.ds(h * HD, HD)
         for b in range(n):
             cols = pl.ds(b * size, size)
             dm = dm_s[rows, cols]
@@ -119,18 +118,21 @@
             acc[0, rows, cols] = dot(qkv_s[1, rows, cols], ds)
             acc[1, rows, cols] = dot(qkv_s[0, rows, cols], ds, NT)
             acc[2, rows, cols] = dot(dm, p.astype(BF16), NT)
-        return 0
-
-    for k, step in enumerate(between):
-        lax.fori_loop(k * HEADS // len(between), (k + 1) * HEADS // len(between), head, 0)
-        step()
-    hat, scale = norm(x.astype(F32))
-    normed = hat.astype(BF16)
+
+    for h in range(HEADS):
+        head(h)
+        between.get(h, lambda: None)()
+
+
+def weights_back(normed, d_s, grads, first):
+    for t in range(3):
+        put(grads, first + t, dot(normed, d_s[t], TN))
+
+
+def input_back(hat, scale, g, d_s, qkv):
     dn = None
     for t in range(3):
-        d = acc[t].T.astype(BF16)
-        put(grads, first + t, dot(normed, d, TN))
-        part = dot(d, qkv[:, t * E:(t + 1) * E], NT)
+        part = dot(d_s[t], qkv[:, t * E:(t + 1) * E], NT)
         dn = part if dn is None else dn + part
     return (g.astype(F32) + norm_back(hat, scale, dn.astype(BF16).astype(F32))).astype(BF16)
 
@@ -184,7 +186,7 @@
         copy.wait()
 
 
-def total_steps(buf, out, first, count, r1, r2, r3, s1, s2, sems):
+def total_steps(buf, out, first, count, r1, r2, s1, sems):
     rec, attr = lax.axis_index("rec"), lax.axis_index("attr")
     n_rec, n_x = lax.axis_size("rec"), lax.axis_size("attr") // 2
     half, x = lax.rem(attr, 2), lax.div(attr, 2)
@@ -203,37 +205,27 @@
         return copy
 
     partner = {"attr": x * 2 + 1 - half}
-    columns = [lax.rem(x + d, n_x) for d in range(1, n_x)]
-    lines = [lax.rem(rec + d, n_rec) for d in range(1, n_rec)]
+    chips = [
+        (lax.rem(rec + d, n_rec), lax.rem(x + c, n_x)) for d, c in np.ndindex(n_rec, n_x) if d or c
+    ]
     copies = [push(buf.at[pl.ds(first + (1 - half) * h1, h1)], r1, partner)]
     yield
     settle(copies)
     for b in range(h1):
         s1[b] = (buf[first + half * h1 + b].astype(F32) + r1[b].astype(F32)).astype(BF16)
     copies = [
-        push(s1.at[pl.ds(c * h2, h2)], r2.at[d], {"attr": c * 2 + half}) for d, c in enumerate(columns)
+        push(s1.at[pl.ds(c * h2, h2), r], r2.at[k], {"rec": r, "attr": c * 2 + half})
+        for k, (r, c) in enumerate(chips)
     ]
     yield
     settle(copies)
     for b in range(h2):
-        value = s1[x * h2 + b].astype(F32)
-        for d in range(n_x - 1):
-            value += r2[d, b].astype(F32)
-        s2[b] = value.astype(BF16)
-    copies = [push(s2.at[:, r], r3.at[d], {"rec": r}) for d, r in enumerate(lines)]
-    yield
-    settle(copies)
-    for b in range(h2):
-        value = s2[b, rec].astype(F32)
-        for d in range(n_rec - 1):
-            value += r3[d, b].astype(F32)
+        value = s1[x * h2 + b, rec].astype(F32)
+        for k in range(len(chips)):
+            value += r2[k, b].astype(F32)
         out[base + b, rec] = value.astype(BF16)
     own = out.at[pl.ds(base, h2), rec]
-    copies = [push(own, own, {"rec": r}) for r in lines]
-    yield
-    settle(copies)
-    own = out.at[pl.ds(base, h2)]
-    copies = [push(own, own, {"attr": c * 2 + half}) for c in columns]
+    copies = [push(own, own, {"rec": r, "attr": c * 2 + half}) for r, c in chips]
     yield
     settle(copies)
     own = out.at[pl.ds(first + half * h1, h1)]
@@ -243,7 +235,9 @@
     yield
 
 
-COUNTS = (8, 4, 4)
+COUNTS = (4, 4, 4, 4)
+UP = (0, 1, 4, 5)
+DOWN = (2, 3, 6, 7)
 
 
 def layer_kernel(
@@ -252,7 +246,7 @@
     o_got, totals,
     cells, cot, qkva, outa, qkvs, outs, up, down, split, places, in_sems,
     flat, c_send, c_got, g_send, g_got, f_send, f_got, b_send, b_got, o_send,
-    x_a, mixed_a, qkv_a, p_a, x_s, g_s, qkv_s, p_s, acc, dm_s, dn_s, bias, grads,
+    x_a, mixed_a, qkv_a, p_a, x_s, g_s, qkv_s, p_s, acc, d_s, dm_s, dn_s, bias, grads,
     c_sems, g_sems, f_sems, b_sems, o_sems, *sums,
 ):
     tokens = flat.shape[0]
@@ -304,6 +298,10 @@
     settle(f_copies)
     x_s[...] = moved(at(3), unpack(f_got, flat, few)).astype(BF16)
     _, mixed, second = attend(x_s, qkvs, outs[...], qkv_s, p_s, acc, n_s, size_s, bias)
+    starts = [sum(COUNTS[:k]) for k in range(4)]
+    ffn1, ffn2, samp, attr = (
+        total_steps(grads, totals, starts[k], COUNTS[k], *sums[4 * k:4 * k + 4]) for k in range(4)
+    )
     hat, scale = norm(second.astype(F32))
     normed = hat.astype(BF16)
     g = g_s[...]
@@ -315,18 +313,17 @@
         slope = cdf + pre * (jnp.exp(pre * pre * -0.5) * (1.0 / math.sqrt(2.0 * math.pi)))
         dh = dot(g, down[:, c * E:(c + 1) * E]).astype(BF16).astype(F32)
         dpre = (dh * slope).astype(BF16)
-        put(grads, c, dot(normed, dpre, TN))
-        put(grads, 4 + c, dot(g, hidden, TN))
+        put(grads, UP[c], dot(normed, dpre, TN))
+        put(grads, DOWN[c], dot(g, hidden, TN))
         part = dot(dpre, w_up, NT)
         if c == 0:
             dn_s[...] = part
         else:
             dn_s[...] += part
-    starts = (0, COUNTS[0], COUNTS[0] + COUNTS[1])
-    ffn, samp, attr = (
-        total_steps(grads, totals, starts[k], COUNTS[k], *sums[6 * k:6 * k + 6]) for k in range(3)
-    )
-    next(ffn)
+        if c == 1:
+            next(ffn1)
+    next(ffn2)
+    next(ffn1)
     dn = dn_s[...].astype(BF16).astype(F32)
     g = (g.astype(F32) + norm_back(hat, scale, dn)).astype(BF16)
 
@@ -336,24 +333,34 @@
                 next(group)
         return step
 
-    back = attend_back(
-        x_s[...], g, mixed, qkvs, outs[...], qkv_s, p_s, acc, dm_s, grads, starts[1], n_s, size_s,
-        (go(ffn), go(), go(ffn)),
-    )
+    heads_back(
+        g, outs[...], qkv_s, p_s, acc, dm_s, n_s, size_s, {1: go(ffn2)},
+    )
+    hat, scale = norm(x_s[...].astype(F32))
+    for t in range(3):
+        d_s[t] = acc[t].T.astype(BF16)
+    back = input_back(hat, scale, g, d_s, qkvs)
     pack(b_send, moved(at(5), back), few)
     b_copies = start_swap(("rec", "attr"), b_send, b_got, b_sems)
-    next(samp)
+    next(ffn1)
+    put(grads, starts[2] + 3, dot(mixed, g, TN))
+    weights_back(hat.astype(BF16), d_s, grads, starts[2])
+    go(samp, samp, ffn2)()
     settle(b_copies)
-    go(samp, ffn)()
     g = moved(at(6), unpack(b_got, flat, few)).astype(BF16)
-    back = attend_back(
-        x_a[...], g, mixed_a[...], qkva, outa[...], qkv_a, p_a, acc, dm_s, grads, starts[2], n_a, size_a,
-        (go(ffn), go(samp), go(ffn)),
-    )
+    put(grads, starts[3] + 3, dot(mixed_a[...], g, TN))
+    heads_back(
+        g, outa[...], qkv_a, p_a, acc, dm_s, n_a, size_a, {2: go(ffn1), 4: go(samp), 5: go(ffn2)},
+    )
+    hat, scale = norm(x_a[...].astype(F32))
+    for t in range(3):
+        d_s[t] = acc[t].T.astype(BF16)
+    weights_back(hat.astype(BF16), d_s, grads, starts[3])
     next(attr)
+    back = input_back(hat, scale, g, d_s, qkva)
     pack(o_send, back.astype(F32), few)
     o_copies = start_swap(("attr",), o_send, o_got, o_sems)
-    for steps in (samp, attr, ffn, samp, attr, samp, attr, samp, attr, attr, attr):
+    for steps in (attr, ffn1, ffn2, samp, attr, samp, attr, attr):
         next(steps)
     settle(o_copies)
 
@@ -384,8 +391,8 @@
         side = tmp[b]
         return jnp.concatenate([side[:, :E], side[:, E:]], axis=0)
 
-    gu[...] = jnp.concatenate([block(c) for c in range(4)], axis=1)
-    gd[...] = jnp.concatenate([block(4 + c) for c in range(4)], axis=1)
+    gu[...] = jnp.concatenate([block(c) for c in UP], axis=1)
+    gd[...] = jnp.concatenate([block(c) for c in DOWN], axis=1)
     for ref, start in ((qs, 8), (qa, 12)):
         ref[...] = jnp.concatenate([block(start + t) for t in range(3)], axis=1)
     os[...] = block(11)
@@ -436,10 +443,8 @@
         h1 = count // 2
         h2 = h1 // n_x
         sums += [
-            vmem(h1, n_rec, part, 2 * E), vmem(max(1, n_x - 1), h2, n_rec, part, 2 * E),
-            vmem(max(1, n_rec - 1), h2, part, 2 * E), vmem(h1, n_rec, part, 2 * E),
-            vmem(h2, n_rec, part, 2 * E),
-            pltpu.SemaphoreType.DMA((2, 2 * (n_rec + n_x - 1))),
+            vmem(h1, n_rec, part, 2 * E), vmem(n_rec * n_x - 1, h2, part, 2 * E),
+            vmem(h1, n_rec, part, 2 * E), pltpu.SemaphoreType.DMA((2, 2 * n_rec * n_x)),
         ]
     o_got, totals = pl.pallas_call(
         functools.partial(layer_kernel, width, size, length, few),
@@ -452,7 +457,7 @@
             vmem(tokens, E, dtype=F32), c_buf, c_buf, g_buf, g_buf, f_buf, f_buf, f_buf, f_buf, c_buf,
             table, table, vmem(3, E, tokens), vmem(tokens // width, HEADS, width, width, dtype=F32),
             table, table, vmem(3, E, tokens), vmem(tokens // size, HEADS, size, size, dtype=F32),
-            vmem(3, E, tokens, dtype=F32), vmem(E, tokens), vmem(tokens, E, dtype=F32),
+            vmem(3, E, tokens, dtype=F32), vmem(3, tokens, E), vmem(E, tokens), vmem(tokens, E, dtype=F32),
             vmem(size, size, dtype=F32), vmem(BLOCKS, n_rec, part, 2 * E),
         ]
         + [

time: 81.5 us -> 72.3 us (0.89)
  Pallas kernels: 80.6 us -> 71.3 us
    pallas_call x1, Pallas kernels: 77.3 us -> 68.1 us  [local(): pl.pallas_call(functools.partial(layer_kernel, width, size, length, few),...]
where the time goes in v1:
time: 72.3 us; the launch traced here: 72.1 us
  Pallas kernels  71.3 us (99%)
  between operations  0.8 us (1%)
    pallas_call x1, Pallas kernels, local(): pl.pallas_call(functools.partial(layer_kernel, width, size, length, few),...  68.1 us
    pallas_call x1, Pallas kernels, local(): pl.pallas_call(functools.partial(finish_kernel, 1.0 / math.sqrt(length *...  3.25 us

profile of v1, /device:TPU:0, one launch (start us, length us, event | category | flops | bytes accessed | tf_op | source)
XLA Modules:
  0.0 72.1 jit_solution(5331065384181787476)
XLA Ops:
  0.6 68.1 %shard_map.153 = (bf16[4,64,384]{2,1,0:T(8,128)(2,1)}, bf16[16,4,24,384]{3,2,1,0:T(8,128)(2,1)}) custom-call(bf16[8,12288]{1,0:T(8,128)(2,1)} %cells_h.1, bf16[8,12288]{1,0:T(8,128)(2,1)} %cot_h.1, bf16[192,576]{1,0:T(8,128)(2,1)} %qkva_h.1, bf16[192,192]{1,0:T(8,128)(2,1)} %outa_h.1, bf16[192,576]{1,0:T(8,128)(2,1)} %qkvs_h.1, bf16[192,192]{1,0:T(8,128)(2,1)} %outs_h.1, ...), custom_call_target="tpu_custom_call" | custom-call | tf_op jit(solution)/shard_map/pallas_call | solution.py:449
  68.7 3.2 %shard_map.154 = (bf16[8,12288]{1,0:T(8,128)(2,1)}, f32[192,576]{1,0:T(8,128)}, f32[192,192]{1,0:T(8,128)}, f32[192,576]{1,0:T(8,128)}, f32[192,192]{1,0:T(8,128...) custom-call(bf16[4,64,384]{2,1,0:T(8,128)(2,1)} %get-tuple-element.16.tokens_h, s32[8,512]{1,0:T(8,128)} %constant.2.clone.place_h.places_h, ...), custom_call_target="tpu_custom_call" | custom-call | tf_op jit(solution)/shard_map/pallas_call | solution.py:478

commit v2 on v1

--- a/solution.py
+++ b/solution.py
@@ -36,10 +36,14 @@
     return there.astype(np.int32)
 
 
+def mover(where_ref):
+    n = where_ref.shape[1]
+    hot = lax.broadcasted_iota(jnp.int32, (n, n), 0) == where_ref[...]
+    return jnp.where(hot, 1.0, 0.0).astype(BF16)
+
+
 def moved(where_ref, x):
-    n = x.shape[0]
-    hot = lax.broadcasted_iota(jnp.int32, (n, n), 0) == where_ref[...]
-    return dot(jnp.where(hot, 1.0, 0.0).astype(BF16), x)
+    return dot(mover(where_ref), x)
 
 
 def put(ref, b, value):
@@ -81,8 +85,11 @@
     )
 
 
-def attend(x_ref, qkv, out, qkv_s, p_s, acc, n, size, bias):
-    normed = norm(x_ref[...].astype(F32))[0].astype(BF16)
+def attend(x_ref, qkv, out, qkv_s, p_s, acc, n, size, bias, kept):
+    hat, scale = norm(x_ref[...].astype(F32))
+    normed = hat.astype(BF16)
+    if kept is not None:
+        kept[0][...], kept[1][...] = hat, scale
     for t in range(3):
         qkv_s[t] = dot(normed, qkv[:, t * E:(t + 1) * E]).T.astype(BF16)
 
@@ -186,7 +193,7 @@
         copy.wait()
 
 
-def total_steps(buf, out, first, count, r1, r2, s1, sems):
+def total_steps(wide, saves, kept, save_sem, buf, out, first, count, r1, r2, s1, sems):
     rec, attr = lax.axis_index("rec"), lax.axis_index("attr")
     n_rec, n_x = lax.axis_size("rec"), lax.axis_size("attr") // 2
     half, x = lax.rem(attr, 2), lax.div(attr, 2)
@@ -225,17 +232,29 @@
             value += r2[k, b].astype(F32)
         out[base + b, rec] = value.astype(BF16)
     own = out.at[pl.ds(base, h2), rec]
-    copies = [push(own, own, {"rec": r, "attr": c * 2 + half}) for r, c in chips]
+    if wide:
+        copies = [push(own, own, {"rec": r, "attr": c * 2 + half}) for r, c in chips]
+    else:
+        copies = [push(own, own, {"rec": lax.rem(rec + d, n_rec)}) for d in range(1, n_rec)]
+        yield
+        settle(copies)
+        own = out.at[pl.ds(base, h2)]
+        copies = [push(own, own, {"attr": lax.rem(x + c, n_x) * 2 + half}) for c in range(1, n_x)]
     yield
     settle(copies)
     own = out.at[pl.ds(first + half * h1, h1)]
     copies = [push(own, own, partner)]
     yield
     settle(copies)
+    group = pl.ds(first, count)
+    save = pltpu.make_async_copy(out.at[group], kept.at[group], save_sem)
+    save.start()
+    saves.append(save)
     yield
 
 
 COUNTS = (4, 4, 4, 4)
+KEPT = (2, 3, 5, 6)
 UP = (0, 1, 4, 5)
 DOWN = (2, 3, 6, 7)
 
@@ -243,10 +262,10 @@
 def layer_kernel(
     size_a, size_s, length, few,
     cells_h, cot_h, qkva_h, outa_h, qkvs_h, outs_h, up_h, down_h, split_h, place_h,
-    o_got, totals,
-    cells, cot, qkva, outa, qkvs, outs, up, down, split, places, in_sems,
+    o_h, totals_h,
+    o_got, totals, save_sems, cells, cot, qkva, outa, qkvs, outs, up, down, split, places, in_sems,
     flat, c_send, c_got, g_send, g_got, f_send, f_got, b_send, b_got, o_send,
-    x_a, mixed_a, qkv_a, p_a, x_s, g_s, qkv_s, p_s, acc, d_s, dm_s, dn_s, bias, grads,
+    x_a, mixed_a, qkv_a, p_a, x_s, g_s, qkv_s, p_s, acc, d_s, dm_s, dn_s, hat_s, scale_s, hots, bias, grads,
     c_sems, g_sems, f_sems, b_sems, o_sems, *sums,
 ):
     tokens = flat.shape[0]
@@ -277,11 +296,13 @@
     g_copies = start_swap(("rec",), g_send, g_got, g_sems)
     for k in range(3, len(pairs)):
         loads[k].wait()
+    for k, i in enumerate(KEPT):
+        hots[k] = mover(at(i))
     settle(c_copies)
     x_a[...] = unpack(c_got, flat, few)
-    _, mixed, first = attend(x_a, qkva, outa[...], qkv_a, p_a, acc, n_a, size_a, None)
+    _, mixed, first = attend(x_a, qkva, outa[...], qkv_a, p_a, acc, n_a, size_a, None, None)
     mixed_a[...] = mixed
-    pack(f_send, moved(at(2), first), few)
+    pack(f_send, dot(hots[0], first), few)
     f_copies = start_swap(("rec", "attr"), f_send, f_got, f_sems)
 
     row = lax.broadcasted_iota(jnp.int32, (size_s, size_s), 0)
@@ -296,11 +317,12 @@
     settle(g_copies)
     g_s[...] = moved(at(4), unpack(g_got, flat, few)).astype(BF16)
     settle(f_copies)
-    x_s[...] = moved(at(3), unpack(f_got, flat, few)).astype(BF16)
-    _, mixed, second = attend(x_s, qkvs, outs[...], qkv_s, p_s, acc, n_s, size_s, bias)
+    x_s[...] = dot(hots[1], unpack(f_got, flat, few)).astype(BF16)
+    _, mixed, second = attend(x_s, qkvs, outs[...], qkv_s, p_s, acc, n_s, size_s, bias, (hat_s, scale_s))
+    saves = []
     starts = [sum(COUNTS[:k]) for k in range(4)]
     ffn1, ffn2, samp, attr = (
-        total_steps(grads, totals, starts[k], COUNTS[k], *sums[4 * k:4 * k + 4]) for k in range(4)
+        total_steps(k > 1, saves, totals_h, save_sems.at[k], grads, totals, starts[k], COUNTS[k], *sums[4 * k:4 * k + 4]) for k in range(4)
     )
     hat, scale = norm(second.astype(F32))
     normed = hat.astype(BF16)
@@ -336,53 +358,58 @@
     heads_back(
         g, outs[...], qkv_s, p_s, acc, dm_s, n_s, size_s, {1: go(ffn2)},
     )
-    hat, scale = norm(x_s[...].astype(F32))
     for t in range(3):
         d_s[t] = acc[t].T.astype(BF16)
-    back = input_back(hat, scale, g, d_s, qkvs)
-    pack(b_send, moved(at(5), back), few)
+    back = input_back(hat_s[...], scale_s[...], g, d_s, qkvs)
+    pack(b_send, dot(hots[2], back), few)
     b_copies = start_swap(("rec", "attr"), b_send, b_got, b_sems)
-    next(ffn1)
     put(grads, starts[2] + 3, dot(mixed, g, TN))
-    weights_back(hat.astype(BF16), d_s, grads, starts[2])
-    go(samp, samp, ffn2)()
+    weights_back(hat_s[...].astype(BF16), d_s, grads, starts[2])
+    go(samp, ffn1, samp, ffn2)()
+    hat_s[...], scale_s[...] = norm(x_a[...].astype(F32))
     settle(b_copies)
-    g = moved(at(6), unpack(b_got, flat, few)).astype(BF16)
+    g = dot(hots[3], unpack(b_got, flat, few)).astype(BF16)
     put(grads, starts[3] + 3, dot(mixed_a[...], g, TN))
     heads_back(
-        g, outa[...], qkv_a, p_a, acc, dm_s, n_a, size_a, {2: go(ffn1), 4: go(samp), 5: go(ffn2)},
+        g, outa[...], qkv_a, p_a, acc, dm_s, n_a, size_a, {1: go(ffn1), 2: go(samp), 3: go(ffn2), 5: go(ffn1)},
     )
-    hat, scale = norm(x_a[...].astype(F32))
     for t in range(3):
         d_s[t] = acc[t].T.astype(BF16)
+    hat = hat_s[...]
     weights_back(hat.astype(BF16), d_s, grads, starts[3])
     next(attr)
-    back = input_back(hat, scale, g, d_s, qkva)
+    back = input_back(hat, scale_s[...], g, d_s, qkva)
     pack(o_send, back.astype(F32), few)
     o_copies = start_swap(("attr",), o_send, o_got, o_sems)
-    for steps in (attr, ffn1, ffn2, samp, attr, samp, attr, attr):
+
+    def cells_back():
+        settle(o_copies)
+        save = pltpu.make_async_copy(o_got, o_h, save_sems.at[len(COUNTS)])
+        save.start()
+        saves.append(save)
+        yield
+
+    cells_out = cells_back()
+    for steps in (attr, ffn2, ffn1, samp, attr, ffn2, samp, cells_out, attr, attr):
         next(steps)
-    settle(o_copies)
+    for save in saves:
+        save.wait()
 
 
 def finish_kernel(
-    factor, few, tokens_h, places_h, total_h, cells, qa, oa, qs, os, gu, gd,
-    tokens, places, total, sems, flat, out_flat, tmp,
+    factor, few, tokens_h, places_h, total_h, cells_h, qa_h, oa_h, qs_h, os_h, gu_h, gd_h,
+    tokens, places, total, cells, qa, oa, qs, os, gu, gd, sems, out_sems, flat, out_flat, tmp,
 ):
     loads = [
         pltpu.make_async_copy(src, dst, sems.at[k])
-        for k, (src, dst) in enumerate(((tokens_h, tokens), (places_h, places), (total_h, total)))
+        for k, (src, dst) in enumerate(
+            [(total_h.at[pl.ds(4 * k, 4)], total.at[pl.ds(4 * k, 4)]) for k in range(4)]
+            + [(places_h, places), (tokens_h, tokens)]
+        )
     ]
     for load in loads:
         load.start()
     rows = cells.shape[0]
-    loads[0].wait()
-    loads[1].wait()
-    out_flat[...] = moved(places.at[7:8], unpack(tokens, flat, few))
-    for a in range(0, cells.shape[1] // E, 2):
-        pair = [out_flat[(a + k) * rows:(a + k + 1) * rows] for k in range(2)]
-        cells[:, a * E:(a + 2) * E] = jnp.concatenate(pair, axis=1).astype(BF16)
-    loads[2].wait()
 
     def block(b):
         part = total.shape[2]
@@ -391,12 +418,34 @@
         side = tmp[b]
         return jnp.concatenate([side[:, :E], side[:, E:]], axis=0)
 
+    stores = []
+
+    def store(src, dst):
+        copy = pltpu.make_async_copy(src, dst, out_sems.at[len(stores)])
+        copy.start()
+        stores.append(copy)
+
+    loads[0].wait()
+    loads[1].wait()
     gu[...] = jnp.concatenate([block(c) for c in UP], axis=1)
+    store(gu, gu_h)
     gd[...] = jnp.concatenate([block(c) for c in DOWN], axis=1)
-    for ref, start in ((qs, 8), (qa, 12)):
-        ref[...] = jnp.concatenate([block(start + t) for t in range(3)], axis=1)
-    os[...] = block(11)
-    oa[...] = block(15)
+    store(gd, gd_h)
+    for ref, dst, side, side_h, k in ((qs, qs_h, os, os_h, 2), (qa, qa_h, oa, oa_h, 3)):
+        loads[k].wait()
+        ref[...] = jnp.concatenate([block(4 * k + t) for t in range(3)], axis=1)
+        store(ref, dst)
+        side[...] = block(4 * k + 3)
+        store(side, side_h)
+    loads[4].wait()
+    loads[5].wait()
+    out_flat[...] = moved(places.at[7:8], unpack(tokens, flat, few))
+    for a in range(0, cells.shape[1] // E, 2):
+        pair = [out_flat[(a + k) * rows:(a + k + 1) * rows] for k in range(2)]
+        cells[:, a * E:(a + 2) * E] = jnp.concatenate(pair, axis=1).astype(BF16)
+    store(cells, cells_h)
+    for copy in stores:
+        copy.wait()
 
 
 def local(
@@ -450,14 +499,18 @@
         functools.partial(layer_kernel, width, size, length, few),
         out_shape=[shape(n_attr, cols, few * E), shape(BLOCKS, n_rec, part, 2 * E)],
         in_specs=[HBM] * len(args),
-        out_specs=[VMEM] * 2,
-        scratch_shapes=[pltpu.VMEM(a.shape, a.dtype) for a in args]
+        out_specs=[HBM] * 2,
+        scratch_shapes=[
+            c_buf, vmem(BLOCKS, n_rec, part, 2 * E), pltpu.SemaphoreType.DMA((len(COUNTS) + 1,)),
+        ]
+        + [pltpu.VMEM(a.shape, a.dtype) for a in args]
         + [
             pltpu.SemaphoreType.DMA((len(args),)),
             vmem(tokens, E, dtype=F32), c_buf, c_buf, g_buf, g_buf, f_buf, f_buf, f_buf, f_buf, c_buf,
             table, table, vmem(3, E, tokens), vmem(tokens // width, HEADS, width, width, dtype=F32),
             table, table, vmem(3, E, tokens), vmem(tokens // size, HEADS, size, size, dtype=F32),
             vmem(3, E, tokens, dtype=F32), vmem(3, tokens, E), vmem(E, tokens), vmem(tokens, E, dtype=F32),
+            vmem(tokens, E, dtype=F32), vmem(tokens, 1, dtype=F32), vmem(len(KEPT), tokens, tokens),
             vmem(size, size, dtype=F32), vmem(BLOCKS, n_rec, part, 2 * E),
         ]
         + [
@@ -479,10 +532,10 @@
         functools.partial(finish_kernel, 1.0 / math.sqrt(length * width), few),
         out_shape=outs,
         in_specs=[ANY] * 3,
-        out_specs=[VMEM] * len(outs),
-        scratch_shapes=[pltpu.VMEM(a.shape, a.dtype) for a in last]
+        out_specs=[ANY] * len(outs),
+        scratch_shapes=[pltpu.VMEM(a.shape, a.dtype) for a in (*last, *outs)]
         + [
-            pltpu.SemaphoreType.DMA((3,)), vmem(tokens, E, dtype=F32), vmem(tokens, E, dtype=F32),
+            pltpu.SemaphoreType.DMA((6,)), pltpu.SemaphoreType.DMA((len(outs),)), vmem(tokens, E, dtype=F32), vmem(tokens, E, dtype=F32),
             vmem(BLOCKS, E // 2, 2 * E, dtype=F32),
         ],
         compiler_params=pltpu.CompilerParams(vmem_limit_bytes=67043328),

time: 72.3 us -> 71.2 us (0.985)
  Pallas kernels: 71.3 us -> 70.2 us
    pallas_call x1, Pallas kernels: 68.1 us -> 67 us  [local(): pl.pallas_call(functools.partial(layer_kernel, width, size, length, few),...]
where the time goes in v2:
time: 71.2 us; the launch traced here: 71 us
  Pallas kernels  70.2 us (99%)
  between operations  0.8 us (1%)
    pallas_call x1, Pallas kernels, local(): pl.pallas_call(functools.partial(layer_kernel, width, size, length, few),...  67 us
    pallas_call x1, Pallas kernels, local(): pl.pallas_call(functools.partial(finish_kernel, 1.0 / math.sqrt(length *...  3.22 us

profile of v2, /device:TPU:0, one launch (start us, length us, event | category | flops | bytes accessed | tf_op | source)
XLA Modules:
  0.0 71.0 jit_solution(14806344116068490444)
XLA Ops:
  0.6 67.0 %shard_map.153 = (bf16[4,64,384]{2,1,0:T(8,128)(2,1)}, bf16[16,4,24,384]{3,2,1,0:T(8,128)(2,1)}) custom-call(bf16[8,12288]{1,0:T(8,128)(2,1)} %cells_h.1, bf16[8,12288]{1,0:T(8,128)(2,1)} %cot_h.1, bf16[192,576]{1,0:T(8,128)(2,1)} %qkva_h.1, bf16[192,192]{1,0:T(8,128)(2,1)} %outa_h.1, bf16[192,576]{1,0:T(8,128)(2,1)} %qkvs_h.1, bf16[192,192]{1,0:T(8,128)(2,1)} %outs_h.1, ...), custom_call_target="tpu_custom_call" | custom-call | tf_op jit(solution)/shard_map/pallas_call | solution.py:498
  67.6 3.2 %shard_map.154 = (bf16[8,12288]{1,0:T(8,128)(2,1)}, f32[192,576]{1,0:T(8,128)}, f32[192,192]{1,0:T(8,128)}, f32[192,576]{1,0:T(8,128)}, f32[192,192]{1,0:T(8,128...) custom-call(bf16[4,64,384]{2,1,0:T(8,128)(2,1)} %get-tuple-element.16.tokens_h, s32[8,512]{1,0:T(8,128)} %constant.2.clone.place_h.places_h, ...), custom_call_target="tpu_custom_call" | custom-call | tf_op jit(solution)/shard_map/pallas_call | solution.py:531

commit v3 on v2

--- a/solution.py
+++ b/solution.py
@@ -85,13 +85,13 @@
     )
 
 
-def attend(x_ref, qkv, out, qkv_s, p_s, acc, n, size, bias, kept):
+def attend(x_ref, turned, out, qkv_s, p_s, acc, n, size, bias, kept):
     hat, scale = norm(x_ref[...].astype(F32))
     normed = hat.astype(BF16)
     if kept is not None:
         kept[0][...], kept[1][...] = hat, scale
     for t in range(3):
-        qkv_s[t] = dot(normed, qkv[:, t * E:(t + 1) * E]).T.astype(BF16)
+        qkv_s[t] = dot(turned[t], normed, NT).astype(BF16)
 
     def head(h):
         rows = pl.ds(h * HD, HD)
@@ -107,8 +107,8 @@
 
     for h in range(HEADS):
         head(h)
-    mixed = acc[0].T.astype(BF16)
-    return normed, mixed, (x_ref[...].astype(F32) + dot(mixed, out)).astype(BF16)
+    mixed = acc[0].astype(BF16)
+    return mixed, (x_ref[...].astype(F32) + dot(mixed.T, out)).astype(BF16)
 
 
 def heads_back(g, out, qkv_s, p_s, acc, dm_s, n, size, between):
@@ -133,15 +133,15 @@
 
 def weights_back(normed, d_s, grads, first):
     for t in range(3):
-        put(grads, first + t, dot(normed, d_s[t], TN))
+        put(grads, first + t, dot(normed, d_s[t], NT))
 
 
 def input_back(hat, scale, g, d_s, qkv):
     dn = None
     for t in range(3):
-        part = dot(d_s[t], qkv[:, t * E:(t + 1) * E], NT)
+        part = dot(qkv[:, t * E:(t + 1) * E], d_s[t])
         dn = part if dn is None else dn + part
-    return (g.astype(F32) + norm_back(hat, scale, dn.astype(BF16).astype(F32))).astype(BF16)
+    return (g.astype(F32) + norm_back(hat, scale, dn.astype(BF16).T.astype(F32))).astype(BF16)
 
 
 def rows_of(cells, flat):
@@ -162,6 +162,28 @@
     return [[lax.rem(m + d, n) for m, d, n in zip(me, s, sizes)] for s in shifts]
 
 
+def far_first(axis):
+    n, me = lax.axis_size(axis), lax.axis_index(axis)
+    low = 2 * me < n
+    order = []
+    for i in range(n - 1):
+        down = n - 1 - i
+        to = jnp.where(low, jnp.where(down <= me, down - 1, down), jnp.where(i >= me, i + 1, i))
+        order.append((to, lax.rem(to - me + n, n)))
+    return order
+
+
+def ordered(axes):
+    if axes[0] != "rec":
+        return [(to, k) for k, to in enumerate(peers_of(axes))]
+    if len(axes) == 1:
+        return [([to], d - 1) for to, d in far_first("rec")]
+    rec, attr, n = lax.axis_index("rec"), lax.axis_index("attr"), lax.axis_size("attr")
+    turn = sorted(range(n), key=lambda c: -min(c, n - c))
+    far = [([to, lax.rem(attr + c, n)], d * n + c - 1) for to, d in far_first("rec") for c in turn]
+    return far + [([rec, lax.rem(attr + c, n)], c - 1) for c in turn if c]
+
+
 def start_swap(axes, src, dst, sems):
     _, sizes = shifts_of(axes)
 
@@ -173,7 +195,7 @@
 
     me = flat([lax.axis_index(a) for a in axes])
     copies = []
-    for k, to in enumerate(peers_of(axes)):
+    for to, k in ordered(axes):
         copy = pltpu.make_async_remote_copy(
             src_ref=src.at[flat(to)],
             dst_ref=dst.at[me],
@@ -200,10 +222,8 @@
     h1 = count // 2
     h2 = h1 // n_x
     base = first + half * h1 + x * h2
-    sem = iter(range(sems.shape[1]))
-
-    def push(src, dst, device):
-        k = next(sem)
+
+    def push(src, dst, device, k):
         copy = pltpu.make_async_remote_copy(
             src_ref=src, dst_ref=dst, send_sem=sems.at[0, k], recv_sem=sems.at[1, k],
             device_id=device, device_id_type=MESH,
@@ -212,38 +232,42 @@
         return copy
 
     partner = {"attr": x * 2 + 1 - half}
-    chips = [
-        (lax.rem(rec + d, n_rec), lax.rem(x + c, n_x)) for d, c in np.ndindex(n_rec, n_x) if d or c
-    ]
-    copies = [push(buf.at[pl.ds(first + (1 - half) * h1, h1)], r1, partner)]
+    turn = range(n_x - 1, -1, -1)
+    chips = [(to, lax.rem(x + c, n_x), d * n_x + c) for to, d in far_first("rec") for c in turn]
+    chips += [(rec, lax.rem(x + c, n_x), c) for c in turn if c]
+    many = n_rec * n_x
+    copies = [push(buf.at[pl.ds(first + (1 - half) * h1, h1)], r1, partner, 0)]
     yield
     settle(copies)
     for b in range(h1):
         s1[b] = (buf[first + half * h1 + b].astype(F32) + r1[b].astype(F32)).astype(BF16)
     copies = [
-        push(s1.at[pl.ds(c * h2, h2), r], r2.at[k], {"rec": r, "attr": c * 2 + half})
-        for k, (r, c) in enumerate(chips)
+        push(s1.at[pl.ds(c * h2, h2), r], r2.at[k - 1], {"rec": r, "attr": c * 2 + half}, k)
+        for r, c, k in chips
     ]
     yield
     settle(copies)
     for b in range(h2):
         value = s1[x * h2 + b, rec].astype(F32)
-        for k in range(len(chips)):
+        for k in range(many - 1):
             value += r2[k, b].astype(F32)
         out[base + b, rec] = value.astype(BF16)
     own = out.at[pl.ds(base, h2), rec]
     if wide:
-        copies = [push(own, own, {"rec": r, "attr": c * 2 + half}) for r, c in chips]
+        copies = [push(own, own, {"rec": r, "attr": c * 2 + half}, many - 1 + k) for r, c, k in chips]
     else:
-        copies = [push(own, own, {"rec": lax.rem(rec + d, n_rec)}) for d in range(1, n_rec)]
+        copies = [push(own, own, {"rec": to}, many - 1 + d) for to, d in far_first("rec")]
         yield
         settle(copies)
         own = out.at[pl.ds(base, h2)]
-        copies = [push(own, own, {"attr": lax.rem(x + c, n_x) * 2 + half}) for c in range(1, n_x)]
+        copies = [
+            push(own, own, {"attr": lax.rem(x + c, n_x) * 2 + half}, many + n_rec - 2 + c)
+            for c in range(1, n_x)
+        ]
     yield
     settle(copies)
     own = out.at[pl.ds(first + half * h1, h1)]
-    copies = [push(own, own, partner)]
+    copies = [push(own, own, partner, 2 * many - 1)]
     yield
     settle(copies)
     group = pl.ds(first, count)
@@ -265,7 +289,7 @@
     o_h, totals_h,
     o_got, totals, save_sems, cells, cot, qkva, outa, qkvs, outs, up, down, split, places, in_sems,
     flat, c_send, c_got, g_send, g_got, f_send, f_got, b_send, b_got, o_send,
-    x_a, mixed_a, qkv_a, p_a, x_s, g_s, qkv_s, p_s, acc, d_s, dm_s, dn_s, hat_s, scale_s, hots, bias, grads,
+    x_a, mixed_a, qkv_a, p_a, x_s, g_s, qkv_s, p_s, acc, d_s, dm_s, dn_s, hat_s, scale_s, hots, turned, g_turned, mixed_s, bias, grads,
     c_sems, g_sems, f_sems, b_sems, o_sems, *sums,
 ):
     tokens = flat.shape[0]
@@ -298,9 +322,12 @@
         loads[k].wait()
     for k, i in enumerate(KEPT):
         hots[k] = mover(at(i))
+    for k, w in enumerate((qkva, qkvs)):
+        for t in range(3):
+            turned[k, t] = w[:, t * E:(t + 1) * E].T
     settle(c_copies)
     x_a[...] = unpack(c_got, flat, few)
-    _, mixed, first = attend(x_a, qkva, outa[...], qkv_a, p_a, acc, n_a, size_a, None, None)
+    mixed, first = attend(x_a, turned.at[0], outa[...], qkv_a, p_a, acc, n_a, size_a, None, None)
     mixed_a[...] = mixed
     pack(f_send, dot(hots[0], first), few)
     f_copies = start_swap(("rec", "attr"), f_send, f_got, f_sems)
@@ -316,9 +343,10 @@
     bias[...] = jnp.where(same, tiled, 0.0).T
     settle(g_copies)
     g_s[...] = moved(at(4), unpack(g_got, flat, few)).astype(BF16)
+    g_turned[...] = g_s[...].T
     settle(f_copies)
     x_s[...] = dot(hots[1], unpack(f_got, flat, few)).astype(BF16)
-    _, mixed, second = attend(x_s, qkvs, outs[...], qkv_s, p_s, acc, n_s, size_s, bias, (hat_s, scale_s))
+    mixed_s[...], second = attend(x_s, turned.at[1], outs[...], qkv_s, p_s, acc, n_s, size_s, bias, (hat_s, scale_s))
     saves = []
     starts = [sum(COUNTS[:k]) for k in range(4)]
     ffn1, ffn2, samp, attr = (
@@ -326,6 +354,7 @@
     )
     hat, scale = norm(second.astype(F32))
     normed = hat.astype(BF16)
+    normed_turned = normed.T
     g = g_s[...]
     for c in range(up.shape[1] // E):
         w_up = up[:, c * E:(c + 1) * E]
@@ -335,8 +364,8 @@
         slope = cdf + pre * (jnp.exp(pre * pre * -0.5) * (1.0 / math.sqrt(2.0 * math.pi)))
         dh = dot(g, down[:, c * E:(c + 1) * E]).astype(BF16).astype(F32)
         dpre = (dh * slope).astype(BF16)
-        put(grads, UP[c], dot(normed, dpre, TN))
-        put(grads, DOWN[c], dot(g, hidden, TN))
+        put(grads, UP[c], dot(normed_turned, dpre))
+        put(grads, DOWN[c], dot(g_turned[...], hidden))
         part = dot(dpre, w_up, NT)
         if c == 0:
             dn_s[...] = part
@@ -359,24 +388,25 @@
         g, outs[...], qkv_s, p_s, acc, dm_s, n_s, size_s, {1: go(ffn2)},
     )
     for t in range(3):
-        d_s[t] = acc[t].T.astype(BF16)
+        d_s[t] = acc[t].astype(BF16)
     back = input_back(hat_s[...], scale_s[...], g, d_s, qkvs)
     pack(b_send, dot(hots[2], back), few)
     b_copies = start_swap(("rec", "attr"), b_send, b_got, b_sems)
-    put(grads, starts[2] + 3, dot(mixed, g, TN))
-    weights_back(hat_s[...].astype(BF16), d_s, grads, starts[2])
+    put(grads, starts[2] + 3, dot(mixed_s[...], g))
+    weights_back(hat_s[...].astype(BF16).T, d_s, grads, starts[2])
     go(samp, ffn1, samp, ffn2)()
     hat_s[...], scale_s[...] = norm(x_a[...].astype(F32))
+    g_turned[...] = hat_s[...].astype(BF16).T
     settle(b_copies)
     g = dot(hots[3], unpack(b_got, flat, few)).astype(BF16)
-    put(grads, starts[3] + 3, dot(mixed_a[...], g, TN))
+    put(grads, starts[3] + 3, dot(mixed_a[...], g))
     heads_back(
         g, outa[...], qkv_a, p_a, acc, dm_s, n_a, size_a, {1: go(ffn1), 2: go(samp), 3: go(ffn2), 5: go(ffn1)},
     )
     for t in range(3):
-        d_s[t] = acc[t].T.astype(BF16)
+        d_s[t] = acc[t].astype(BF16)
     hat = hat_s[...]
-    weights_back(hat.astype(BF16), d_s, grads, starts[3])
+    weights_back(g_turned[...], d_s, grads, starts[3])
     next(attr)
     back = input_back(hat, scale_s[...], g, d_s, qkva)
     pack(o_send, back.astype(F32), few)
@@ -507,10 +537,11 @@
         + [
             pltpu.SemaphoreType.DMA((len(args),)),
             vmem(tokens, E, dtype=F32), c_buf, c_buf, g_buf, g_buf, f_buf, f_buf, f_buf, f_buf, c_buf,
-            table, table, vmem(3, E, tokens), vmem(tokens // width, HEADS, width, width, dtype=F32),
+            table, vmem(E, tokens), vmem(3, E, tokens), vmem(tokens // width, HEADS, width, width, dtype=F32),
             table, table, vmem(3, E, tokens), vmem(tokens // size, HEADS, size, size, dtype=F32),
-            vmem(3, E, tokens, dtype=F32), vmem(3, tokens, E), vmem(E, tokens), vmem(tokens, E, dtype=F32),
+            vmem(3, E, tokens, dtype=F32), vmem(3, E, tokens), vmem(E, tokens), vmem(tokens, E, dtype=F32),
             vmem(tokens, E, dtype=F32), vmem(tokens, 1, dtype=F32), vmem(len(KEPT), tokens, tokens),
+            vmem(2, 3, E, E), vmem(E, tokens), vmem(E, tokens),
             vmem(size, size, dtype=F32), vmem(BLOCKS, n_rec, part, 2 * E),
         ]
         + [

time: 71.2 us -> 70.5 us (level)
    pallas_call x1, Pallas kernels: 67 us -> 66.3 us  [local(): pl.pallas_call(functools.partial(layer_kernel, width, size, length, few),...]
where the time goes in v3:
time: 70.5 us; the launch traced here: 70.3 us
  Pallas kernels  69.5 us (99%)
  between operations  0.8 us (1%)
    pallas_call x1, Pallas kernels, local(): pl.pallas_call(functools.partial(layer_kernel, width, size, length, few),...  66.3 us
    pallas_call x1, Pallas kernels, local(): pl.pallas_call(functools.partial(finish_kernel, 1.0 / math.sqrt(length *...  3.22 us

profile of v3, /device:TPU:0, one launch (start us, length us, event | category | flops | bytes accessed | tf_op | source)
XLA Modules:
  0.0 70.3 jit_solution(3784777213712317648)
XLA Ops:
  0.6 66.3 %shard_map.153 = (bf16[4,64,384]{2,1,0:T(8,128)(2,1)}, bf16[16,4,24,384]{3,2,1,0:T(8,128)(2,1)}) custom-call(bf16[8,12288]{1,0:T(8,128)(2,1)} %cells_h.1, bf16[8,12288]{1,0:T(8,128)(2,1)} %cot_h.1, bf16[192,576]{1,0:T(8,128)(2,1)} %qkva_h.1, bf16[192,192]{1,0:T(8,128)(2,1)} %outa_h.1, bf16[192,576]{1,0:T(8,128)(2,1)} %qkvs_h.1, bf16[192,192]{1,0:T(8,128)(2,1)} %outs_h.1, ...), custom_call_target="tpu_custom_call" | custom-call | tf_op jit(solution)/shard_map/pallas_call | solution.py:528
  66.9 3.2 %shard_map.154 = (bf16[8,12288]{1,0:T(8,128)(2,1)}, f32[192,576]{1,0:T(8,128)}, f32[192,192]{1,0:T(8,128)}, f32[192,576]{1,0:T(8,128)}, f32[192,192]{1,0:T(8,128...) custom-call(bf16[4,64,384]{2,1,0:T(8,128)(2,1)} %get-tuple-element.16.tokens_h, s32[8,512]{1,0:T(8,128)} %constant.2.clone.place_h.places_h, ...), custom_call_target="tpu_custom_call" | custom-call | tf_op jit(solution)/shard_map/pallas_call | solution.py:562

commit v4 on v3

--- a/solution.py
+++ b/solution.py
@@ -401,7 +401,7 @@
     g = dot(hots[3], unpack(b_got, flat, few)).astype(BF16)
     put(grads, starts[3] + 3, dot(mixed_a[...], g))
     heads_back(
-        g, outa[...], qkv_a, p_a, acc, dm_s, n_a, size_a, {1: go(ffn1), 2: go(samp), 3: go(ffn2), 5: go(ffn1)},
+        g, outa[...], qkv_a, p_a, acc, dm_s, n_a, size_a, {1: go(ffn1), 2: go(samp), 4: go(ffn2), 5: go(ffn1)},
     )
     for t in range(3):
         d_s[t] = acc[t].astype(BF16)

time: 70.5 us -> 70.3 us (level)
  no operation moved by 1% of the time
where the time goes in v4:
time: 70.3 us; the launch traced here: 70.1 us
  Pallas kernels  69.3 us (99%)
  between operations  0.8 us (1%)
    pallas_call x1, Pallas kernels, local(): pl.pallas_call(functools.partial(layer_kernel, width, size, length, few),...  66.1 us
    pallas_call x1, Pallas kernels, local(): pl.pallas_call(functools.partial(finish_kernel, 1.0 / math.sqrt(length *...  3.22 us

profile of v4, /device:TPU:0, one launch (start us, length us, event | category | flops | bytes accessed | tf_op | source)
XLA Modules:
  0.0 70.1 jit_solution(7930361668747039625)
XLA Ops:
  0.6 66.1 %shard_map.153 = (bf16[4,64,384]{2,1,0:T(8,128)(2,1)}, bf16[16,4,24,384]{3,2,1,0:T(8,128)(2,1)}) custom-call(bf16[8,12288]{1,0:T(8,128)(2,1)} %cells_h.1, bf16[8,12288]{1,0:T(8,128)(2,1)} %cot_h.1, bf16[192,576]{1,0:T(8,128)(2,1)} %qkva_h.1, bf16[192,192]{1,0:T(8,128)(2,1)} %outa_h.1, bf16[192,576]{1,0:T(8,128)(2,1)} %qkvs_h.1, bf16[192,192]{1,0:T(8,128)(2,1)} %outs_h.1, ...), custom_call_target="tpu_custom_call" | custom-call | tf_op jit(solution)/shard_map/pallas_call | solution.py:528
  66.7 3.2 %shard_map.154 = (bf16[8,12288]{1,0:T(8,128)(2,1)}, f32[192,576]{1,0:T(8,128)}, f32[192,192]{1,0:T(8,128)}, f32[192,576]{1,0:T(8,128)}, f32[192,192]{1,0:T(8,128...) custom-call(bf16[4,64,384]{2,1,0:T(8,128)(2,1)} %get-tuple-element.16.tokens_h, s32[8,512]{1,0:T(8,128)} %constant.2.clone.place_h.places_h, ...), custom_call_target="tpu_custom_call" | custom-call | tf_op jit(solution)/shard_map/pallas_call | solution.py:562
